TPU v7x, 32 devices: a whole 2x2x4 slice. The times are simulated.
32 devices in a mesh: roll: 8 (over z, core), kvh: 4 (over y, x).
Axes of the slice: x: 2, y: 2, z: 4, core: 2. Of those that a mesh axis runs over, the one named last changes fastest.
Arguments:
- out_grad: bfloat16 [8, 256, 5120], P('roll', 'kvh'), may hold values from -48 to 48
- out_weight: bfloat16 [4, 5, 128, 5120], P('kvh'), may hold values from -0.078125 to 0.078125
- queries: bfloat16 [8, 256, 4, 5, 128], P('roll', None, 'kvh'), may hold values from -16 to 16
- keys_new: bfloat16 [8, 256, 4, 128], P('roll', None, 'kvh'), may hold values from -16 to 16
- values_new: bfloat16 [8, 256, 4, 128], P('roll', None, 'kvh'), may hold values from -6 to 6
- keys_prompt: bfloat16 [2048, 4, 128], P('roll', 'kvh'), may hold values from -6 to 6
- values_prompt: bfloat16 [2048, 4, 128], P('roll', 'kvh'), may hold values from -6 to 6
- offsets: int32 [8], P('roll'), may hold values from 0 to 3840
Outputs:
- grad_queries: bfloat16 [8, 256, 4, 5, 128], P('roll', None, 'kvh')
- grad_keys_new: bfloat16 [8, 256, 4, 128], P('roll', None, 'kvh')
- grad_values_new: bfloat16 [8, 256, 4, 128], P('roll', None, 'kvh')
- grad_keys_prompt: bfloat16 [2048, 4, 128], P('roll', 'kvh')
- grad_values_prompt: bfloat16 [2048, 4, 128], P('roll', 'kvh')
Inputs may be any that keep to these rules, and one draw needn't show every extreme that they name: `offsets`: each slice lies inside a response of 4096 tokens.
All inputs are finite; a program needn't handle non-finite values.
Results may differ from a plain program's by a relative error of at most 0.015.
The roundings to bfloat16 on the way count: a program that leaves them out, or rounds other values in their place, can miss the bound.
Values may be sent and summed in bfloat16 or wider, within the bound.
No kernel may reach another device: no remote copies, remote signals or barrier semaphores. Data moves between devices by JAX's collectives and lax.ppermute only.
A program may use at most 64 MiB of HBM per device.

v0:
```python
import math
import jax
import jax.numpy as jnp
from jax import lax
from jax.sharding import PartitionSpec as P

theta_base = 1000000.0


def rotation(positions, head_width):
    half_width = head_width // 2
    frequency = jnp.power(theta_base, -(jnp.arange(half_width, dtype=jnp.float32) / half_width))
    angles = positions.astype(jnp.float32)[:, None] * frequency[None, :]
    return (jnp.cos(angles), jnp.sin(angles))


def rotate(vectors, cos_part, sin_part, direction):
    half_width = vectors.shape[-1] // 2
    front_half = vectors[..., :half_width]
    back_half = vectors[..., half_width:]
    return jnp.concatenate(
        [
            front_half * cos_part - direction * back_half * sin_part,
            back_half * cos_part + direction * front_half * sin_part,
        ],
        axis=-1,
    )


def inner_dot(left, right):
    return lax.dot_general(
        left, right, (((1,), (1,)), ((), ())), preferred_element_type=jnp.float32
    )


def outer_sum(left, right):
    return lax.dot_general(
        left, right, (((0,), (0,)), ((), ())), preferred_element_type=jnp.float32
    )


def block_grads(context, key_block, value_block):
    query_rows, grad_rows, log_total, row_delta, score_scale = context
    scores = inner_dot(query_rows, key_block) * score_scale
    attn_probs = jnp.exp(scores - log_total[:, None]).astype(jnp.bfloat16)
    prob_grad = inner_dot(grad_rows, value_block)
    score_grad = (
        attn_probs.astype(jnp.float32) * (prob_grad - row_delta[:, None]) * score_scale
    ).astype(jnp.bfloat16)
    return (attn_probs, score_grad)


def prompt_terms(context, key_rows, value_rows):
    row_count, head_width = key_rows.shape
    block_len = math.gcd(row_count, 512)
    key_blocks = key_rows.reshape(row_count // block_len, block_len, head_width)
    value_blocks = value_rows.reshape(row_count // block_len, block_len, head_width)

    def term_step(unused, blocks):
        attn_probs, score_grad = block_grads(context, blocks[0], blocks[1])
        return (
            unused,
            jnp.stack(
                [outer_sum(score_grad, context[0]), outer_sum(attn_probs, context[1])], axis=1
            ),
        )

    unused, block_terms = lax.scan(
        term_step, jnp.zeros((), jnp.float32), (key_blocks, value_blocks)
    )
    return block_terms.reshape(row_count, 2, head_width)


def local(out_grad, out_weight, queries, keys_new, values_new, keys_prompt, values_prompt, offsets):
    roll_local, seq_len, kv_local, group_size, head_width = queries.shape
    prompt_local = keys_prompt.shape[0]
    prompt_total = prompt_local * lax.axis_size("roll")
    score_scale = head_width ** (-0.5)
    row_total = roll_local * seq_len * group_size
    attn_grad = jnp.einsum(
        "rsc,ghdc->rsghd",
        lax.all_gather(out_grad, "kvh", axis=1, tiled=True),
        out_weight,
        preferred_element_type=jnp.float32,
    ).astype(jnp.bfloat16)
    cached_keys, cached_values = (
        lax.all_gather(keys_prompt, "roll", axis=0, tiled=True),
        lax.all_gather(values_prompt, "roll", axis=0, tiled=True),
    )
    positions = prompt_total + offsets[:, None] + jnp.arange(seq_len, dtype=jnp.int32)[None, :]
    cos_flat, sin_flat = rotation(positions.reshape(-1), head_width)
    cos_four = cos_flat.reshape(roll_local, seq_len, 1, head_width // 2)
    sin_four = sin_flat.reshape(roll_local, seq_len, 1, head_width // 2)
    query_rot = rotate(
        queries.astype(jnp.float32), cos_four[:, :, :, None], sin_four[:, :, :, None], 1.0
    ).astype(jnp.bfloat16)
    key_rot = rotate(keys_new.astype(jnp.float32), cos_four, sin_four, 1.0).astype(jnp.bfloat16)
    block_len = math.gcd(prompt_total, 512)
    block_count = prompt_total // block_len
    causal = (jnp.arange(seq_len)[None, :] <= jnp.arange(seq_len)[:, None])[None, :, None, :]
    head_index = 0
    query_head = query_rot[:, :, head_index]
    key_head = key_rot[:, :, head_index]
    value_head = values_new[:, :, head_index]
    grad_head = attn_grad[:, :, head_index]
    query_rows = query_head.reshape(row_total, head_width)
    grad_rows = grad_head.reshape(row_total, head_width)
    key_blocks = cached_keys[:, head_index].reshape(block_count, block_len, head_width)
    value_blocks = cached_values[:, head_index].reshape(block_count, block_len, head_width)
    near_scores = (
        jnp.einsum("rshd,rtd->rsht", query_head, key_head, preferred_element_type=jnp.float32)
        * score_scale
    )
    near_scores = jnp.where(causal, near_scores, -jnp.inf)
    near_max = jnp.max(near_scores, axis=3, keepdims=True)
    near_sum = jnp.sum(jnp.exp(near_scores - near_max), axis=3)

    def stat_step(running, key_block):
        old_max, old_sum = running
        scores = inner_dot(query_rows, key_block) * score_scale
        new_max = jnp.maximum(old_max, jnp.max(scores, axis=1))
        new_sum = old_sum * jnp.exp(old_max - new_max) + jnp.sum(
            jnp.exp(scores - new_max[:, None]), axis=1
        )
        return ((new_max, new_sum), None)

    stats, unused = lax.scan(
        stat_step, (near_max.reshape(row_total), near_sum.reshape(row_total)), key_blocks
    )
    log_total = stats[0] + jnp.log(stats[1])
    log_shaped = log_total.reshape(roll_local, seq_len, group_size, 1)
    near_probs = jnp.where(causal, jnp.exp(near_scores - log_shaped), 0.0).astype(jnp.bfloat16)
    near_output = jnp.einsum(
        "rsht,rtd->rshd", near_probs, value_head, preferred_element_type=jnp.float32
    ).reshape(row_total, head_width)

    def output_step(total_out, blocks):
        scores = inner_dot(query_rows, blocks[0]) * score_scale
        attn_probs = jnp.exp(scores - log_total[:, None]).astype(jnp.bfloat16)
        return (
            total_out + jnp.dot(attn_probs, blocks[1], preferred_element_type=jnp.float32),
            None,
        )

    output, unused = lax.scan(output_step, near_output, (key_blocks, value_blocks))
    row_delta = jnp.sum(grad_rows.astype(jnp.float32) * output, axis=1)
    context = (query_rows, grad_rows, log_total, row_delta, score_scale)
    contexts = [context]
    near_prob_grad = jnp.einsum(
        "rshd,rtd->rsht", grad_head, value_head, preferred_element_type=jnp.float32
    )
    delta_shaped = row_delta.reshape(roll_local, seq_len, group_size, 1)
    near_grad = (
        near_probs.astype(jnp.float32) * (near_prob_grad - delta_shaped) * score_scale
    ).astype(jnp.bfloat16)
    near_query = jnp.einsum(
        "rsht,rtd->rshd", near_grad, key_head, preferred_element_type=jnp.float32
    )
    key_new_grad = jnp.einsum(
        "rsht,rshd->rtd", near_grad, query_head, preferred_element_type=jnp.float32
    )
    value_new_grad = jnp.einsum(
        "rsht,rshd->rtd", near_probs, grad_head, preferred_element_type=jnp.float32
    )
    zero_rows = jnp.zeros((row_total, head_width), jnp.float32)

    def query_step(total_grad, blocks):
        attn_probs, score_grad = block_grads(context, blocks[0], blocks[1])
        return (
            total_grad + jnp.dot(score_grad, blocks[0], preferred_element_type=jnp.float32),
            None,
        )

    far_query, unused = lax.scan(query_step, zero_rows, (key_blocks, value_blocks))
    query_grad = far_query.reshape(roll_local, seq_len, group_size, head_width) + near_query
    query_list = [rotate(query_grad, cos_four, sin_four, -1.0).astype(jnp.bfloat16)]
    key_list = [
        rotate(key_new_grad, cos_four[:, :, 0], sin_four[:, :, 0], -1.0).astype(jnp.bfloat16)
    ]
    value_list = [value_new_grad.astype(jnp.bfloat16)]
    head_index = 0
    key_rows = cached_keys[:, head_index]
    value_rows = cached_values[:, head_index]
    pieces = [prompt_terms(contexts[head_index], key_rows, value_rows)]
    reduced = lax.psum_scatter(
        jnp.stack(pieces, axis=1).astype(jnp.bfloat16), "roll", scatter_dimension=0, tiled=True
    ).astype(jnp.float32)
    grad_queries = jnp.stack(query_list, axis=2)
    grad_keys_new = jnp.stack(key_list, axis=2)
    grad_values_new = jnp.stack(value_list, axis=2)
    return (
        grad_queries,
        grad_keys_new,
        grad_values_new,
        reduced[:, :, 0].astype(jnp.bfloat16),
        reduced[:, :, 1].astype(jnp.bfloat16),
    )


def solution(mesh):
    placed = (
        P("roll", "kvh", None),
        P("kvh", None, None, None),
        P("roll", None, "kvh", None, None),
        P("roll", None, "kvh", None),
        P("roll", None, "kvh", None),
        P("roll", "kvh", None),
        P("roll", "kvh", None),
        P("roll"),
    )
    return jax.shard_map(
        local,
        mesh=mesh,
        in_specs=placed,
        out_specs=(
            P("roll", None, "kvh", None, None),
            P("roll", None, "kvh", None),
            P("roll", None, "kvh", None),
            P("roll", "kvh", None),
            P("roll", "kvh", None),
        ),
        check_vma=False,
    )
```

profile of v0, /device:TPU:0, one launch (start us, length us, event | category | flops | bytes accessed | tf_op | source)
XLA Modules:
  0.0 133.3 jit_solution(5835152332438345986)
XLA Ops:
  7.2 0.7 all-gather.2.cloned.1.call-update
  8.0 17.7 %all_gather.9 = bf16[2048,1,128]{2,0,1:T(8,128)(2,1)} all-gather(bf16[256,1,128]{2,0,1:T(8,128)(2,1)} %param.21), channel_id=1, replica_groups=mesh['roll'=8,'kvh'=4] {'roll'}, dimensions={0}, use_global_device_ids=true | all-gather | bytes 589824 | tf_op jit(solution)/shard_map/all_gather | solution.py:87
  25.8 1.0 convert_element_type.136
  27.5 0.9 broadcast_multiply_fusion
  29.9 0.6 fusion.96
  30.5 0.6 fusion.103
  32.4 7.5 %while.43 = (s32[]{:T(128)}, f32[1280]{0:T(1024)S(1)}, f32[1280]{0:T(1024)S(1)}, bf16[4,512,128]{2,1,0:T(8,128)(2,1)}, bf16[1280,128]{1,0:T(8,128)(2,1)S(1)}, /*index=5*/s32[]{:T(128)}) while((s32[]{:T(128)}, f32[1280]{0:T(1024)S(1)}, f32[1280]{0:T(1024)S(1)}, bf16[4,512,128]{2,1,0:T(8,128)(2,1)}, bf16[1280,128]{1,0:T(8,128)(2,1)S(1)}, ...), condition=%wide.region_5.6_spmd, body=%wide.region_2.5_spmd.sunk | while | flops 170396160 | bytes 5768273 | solution.py:127
  32.4 1.4 %fusion.141 = (f32[1280]{0:T(1024)S(1)}, f32[512,1280]{1,0:T(8,128)S(1)}) fusion(bf16[1280,128]{1,0:T(8,128)(2,1)S(1)} %get-tuple-element.458, bf16[4,512,128]{2,1,0:T(8,128)(2,1)} %get-tuple-element.457, s32[]{:T(128)S(6)} %copy.79), kind=kOutput, calls=%fused_computation.131.clone.1 | convolution fusion | flops 169081600 | bytes 3085316 | tf_op jit(solution)/shard_map/while/body/eval_jaxpr/dot_general | solution.py:31
  34.3 1.4 %fusion.141 = (f32[1280]{0:T(1024)S(1)}, f32[512,1280]{1,0:T(8,128)S(1)}) fusion(bf16[1280,128]{1,0:T(8,128)(2,1)S(1)} %get-tuple-element.458, bf16[4,512,128]{2,1,0:T(8,128)(2,1)} %get-tuple-element.457, s32[]{:T(128)S(6)} %copy.79), kind=kOutput, calls=%fused_computation.131.clone.1 | convolution fusion | flops 169081600 | bytes 3085316 | tf_op jit(solution)/shard_map/while/body/eval_jaxpr/dot_general | solution.py:31
  36.2 1.4 %fusion.141 = (f32[1280]{0:T(1024)S(1)}, f32[512,1280]{1,0:T(8,128)S(1)}) fusion(bf16[1280,128]{1,0:T(8,128)(2,1)S(1)} %get-tuple-element.458, bf16[4,512,128]{2,1,0:T(8,128)(2,1)} %get-tuple-element.457, s32[]{:T(128)S(6)} %copy.79), kind=kOutput, calls=%fused_computation.131.clone.1 | convolution fusion | flops 169081600 | bytes 3085316 | tf_op jit(solution)/shard_map/while/body/eval_jaxpr/dot_general | solution.py:31
  38.1 1.4 %fusion.141 = (f32[1280]{0:T(1024)S(1)}, f32[512,1280]{1,0:T(8,128)S(1)}) fusion(bf16[1280,128]{1,0:T(8,128)(2,1)S(1)} %get-tuple-element.458, bf16[4,512,128]{2,1,0:T(8,128)(2,1)} %get-tuple-element.457, s32[]{:T(128)S(6)} %copy.79), kind=kOutput, calls=%fused_computation.131.clone.1 | convolution fusion | flops 169081600 | bytes 3085316 | tf_op jit(solution)/shard_map/while/body/eval_jaxpr/dot_general | solution.py:31
  40.6 0.8 copy-done.1
  42.1 16.1 %all_gather.10 = bf16[2048,1,128]{2,0,1:T(8,128)(2,1)} all-gather(bf16[256,1,128]{2,0,1:T(8,128)(2,1)S(1)} %copy-done.14), channel_id=1, replica_groups=mesh['roll'=8,'kvh'=4] {'roll'}, dimensions={0}, use_global_device_ids=true | all-gather | bytes 589824 | tf_op jit(solution)/shard_map/all_gather | solution.py:88
  58.6 7.8 %while.44 = (s32[]{:T(128)}, f32[1280,128]{1,0:T(8,128)S(1)}, bf16[4,512,128]{2,1,0:T(8,128)(2,1)}, bf16[1280,128]{1,0:T(8,128)(2,1)S(1)}, f32[1280]{0:T(1024)S(1)}, /*index=5*/bf16[4,512,128]{2,1,0:T(8,128)(2,1)}, s32[]{:T(128)}) while((s32[]{:T(128)}, f32[1280,128]{1,0:T(8,128)S(1)}, bf16[4,512,128]{2,1,0:T(8,128)(2,1)}, ...), condition=%wide.region_7.8_spmd, body=%wide.region_6.7_spmd.sunk | while | flops 337674240 | bytes 1906773 | solution.py:145
  58.6 1.9 %convolution_add_fusion.5 = f32[1280,128]{1,0:T(8,128)S(1)} fusion(f32[1280,128]{1,0:T(8,128)S(1)} %get-tuple-element.468, bf16[1280,128]{1,0:T(8,128)(2,1)S(1)} %get-tuple-element.477, f32[1280]{0:T(1024)S(1)} %get-tuple-element.478, bf16[4,512,128]{2,1,0:T(8,128)(2,1)} %get-tuple-element.479, s32[]{:T(128)S(6)} %copy.87, ...), kind=kOutput, calls=%fused_computation.10.clone.1 | convolution fusion | flops 337674240 | bytes 1906688 | tf_op jit(solution)/shard_map/while/body/eval_jaxpr/dot_general | solution.py:141
  60.5 1.9 %convolution_add_fusion.5 = f32[1280,128]{1,0:T(8,128)S(1)} fusion(f32[1280,128]{1,0:T(8,128)S(1)} %get-tuple-element.468, bf16[1280,128]{1,0:T(8,128)(2,1)S(1)} %get-tuple-element.477, f32[1280]{0:T(1024)S(1)} %get-tuple-element.478, bf16[4,512,128]{2,1,0:T(8,128)(2,1)} %get-tuple-element.479, s32[]{:T(128)S(6)} %copy.87, ...), kind=kOutput, calls=%fused_computation.10.clone.1 | convolution fusion | flops 337674240 | bytes 1906688 | tf_op jit(solution)/shard_map/while/body/eval_jaxpr/dot_general | solution.py:141
  62.5 1.9 %convolution_add_fusion.5 = f32[1280,128]{1,0:T(8,128)S(1)} fusion(f32[1280,128]{1,0:T(8,128)S(1)} %get-tuple-element.468, bf16[1280,128]{1,0:T(8,128)(2,1)S(1)} %get-tuple-element.477, f32[1280]{0:T(1024)S(1)} %get-tuple-element.478, bf16[4,512,128]{2,1,0:T(8,128)(2,1)} %get-tuple-element.479, s32[]{:T(128)S(6)} %copy.87, ...), kind=kOutput, calls=%fused_computation.10.clone.1 | convolution fusion | flops 337674240 | bytes 1906688 | tf_op jit(solution)/shard_map/while/body/eval_jaxpr/dot_general | solution.py:141
  64.4 1.9 %convolution_add_fusion.5 = f32[1280,128]{1,0:T(8,128)S(1)} fusion(f32[1280,128]{1,0:T(8,128)S(1)} %get-tuple-element.468, bf16[1280,128]{1,0:T(8,128)(2,1)S(1)} %get-tuple-element.477, f32[1280]{0:T(1024)S(1)} %get-tuple-element.478, bf16[4,512,128]{2,1,0:T(8,128)(2,1)} %get-tuple-element.479, s32[]{:T(128)S(6)} %copy.87, ...), kind=kOutput, calls=%fused_computation.10.clone.1 | convolution fusion | flops 337674240 | bytes 1906688 | tf_op jit(solution)/shard_map/while/body/eval_jaxpr/dot_general | solution.py:141
  66.4 5.9 %fusion.67 = bf16[256,5,128]{2,0,1:T(8,128)(2,1)S(1)} fusion(bf16[1,5,128,5120]{3,2,1,0:T(8,128)(2,1)} %param.17, bf16[1,256,5120]{2,1,0:T(8,128)(2,1)} %all-gather.2.cloned.1.call-done), kind=kOutput, calls=%fused_computation.75 | convolution fusion | flops 1677885440 | bytes 9502720 | tf_op jit(solution)/shard_map/rsc,ghdc->rsghd/dot_general | solution.py:80
  72.3 0.7 copy-done.7
  73.7 0.6 copy-done.9
  74.2 15.7 %while.45 = (s32[]{:T(128)}, bf16[4,512,2,128]{3,1,2,0:T(8,128)(2,1)S(1)}, bf16[4,512,128]{2,1,0:T(8,128)(2,1)}, bf16[1280,128]{1,0:T(8,128)(2,1)S(1)}, f32[1280...) while((s32[]{:T(128)}, ...), condition=%wide.region_12.13_spmd, body=%wide.region_11.12_spmd.sunk | while | flops 676855808 | bytes 6301809 | solution.py:68
  74.2 1.5 %fusion.152 = bf16[512,1280]{1,0:T(8,128)(2,1)S(1)} fusion(bf16[1280,128]{1,0:T(8,128)(2,1)S(1)} %get-tuple-element.532, f32[1280]{0:T(1024)S(1)} %get-tuple-element.533, bf16[4,512,128]{2,1,0:T(8,128)(2,1)} %get-tuple-element.531, s32[]{:T(128)S(6)} %copy.99), kind=kOutput, calls=%fused_computation.25.clone.1 | convolution fusion | flops 169738240 | bytes 1774596 | tf_op jit(solution)/shard_map/while/body/eval_jaxpr/dot_general | solution.py:31
  75.7 0.5 convolution_bitcast_fusion.4
  76.2 1.9 %fusion.153 = bf16[512,1,128]{2,0,1:T(8,128)(2,1)S(1)} fusion(bf16[1280,128]{1,0:T(8,128)(2,1)S(1)} %get-tuple-element.532, bf16[1280,128]{1,0:T(8,128)(2,1)S(1)} %get-tuple-element.535, bf16[512,1280]{1,0:T(8,128)(2,1)S(1)} %fusion.152, f32[1280]{0:T(1024)S(1)} %get-tuple-element.536, bf16[4,512,128]{2,1,0:T(8,128)(2,1)} %get-tuple-element.534, ...), kind=kOutput, calls=%fused_computation.30.clone.1 | convolution fusion | flops 338821120 | bytes 2233348 | tf_op jit(solution)/shard_map/while/body/eval_jaxpr/dot_general | solution.py:37
  78.2 1.5 %fusion.152 = bf16[512,1280]{1,0:T(8,128)(2,1)S(1)} fusion(bf16[1280,128]{1,0:T(8,128)(2,1)S(1)} %get-tuple-element.532, f32[1280]{0:T(1024)S(1)} %get-tuple-element.533, bf16[4,512,128]{2,1,0:T(8,128)(2,1)} %get-tuple-element.531, s32[]{:T(128)S(6)} %copy.99), kind=kOutput, calls=%fused_computation.25.clone.1 | convolution fusion | flops 169738240 | bytes 1774596 | tf_op jit(solution)/shard_map/while/body/eval_jaxpr/dot_general | solution.py:31
  80.2 1.9 %fusion.153 = bf16[512,1,128]{2,0,1:T(8,128)(2,1)S(1)} fusion(bf16[1280,128]{1,0:T(8,128)(2,1)S(1)} %get-tuple-element.532, bf16[1280,128]{1,0:T(8,128)(2,1)S(1)} %get-tuple-element.535, bf16[512,1280]{1,0:T(8,128)(2,1)S(1)} %fusion.152, f32[1280]{0:T(1024)S(1)} %get-tuple-element.536, bf16[4,512,128]{2,1,0:T(8,128)(2,1)} %get-tuple-element.534, ...), kind=kOutput, calls=%fused_computation.30.clone.1 | convolution fusion | flops 338821120 | bytes 2233348 | tf_op jit(solution)/shard_map/while/body/eval_jaxpr/dot_general | solution.py:37
  82.1 1.5 %fusion.152 = bf16[512,1280]{1,0:T(8,128)(2,1)S(1)} fusion(bf16[1280,128]{1,0:T(8,128)(2,1)S(1)} %get-tuple-element.532, f32[1280]{0:T(1024)S(1)} %get-tuple-element.533, bf16[4,512,128]{2,1,0:T(8,128)(2,1)} %get-tuple-element.531, s32[]{:T(128)S(6)} %copy.99), kind=kOutput, calls=%fused_computation.25.clone.1 | convolution fusion | flops 169738240 | bytes 1774596 | tf_op jit(solution)/shard_map/while/body/eval_jaxpr/dot_general | solution.py:31
  83.6 0.5 convolution_bitcast_fusion.4
  84.1 1.9 %fusion.153 = bf16[512,1,128]{2,0,1:T(8,128)(2,1)S(1)} fusion(bf16[1280,128]{1,0:T(8,128)(2,1)S(1)} %get-tuple-element.532, bf16[1280,128]{1,0:T(8,128)(2,1)S(1)} %get-tuple-element.535, bf16[512,1280]{1,0:T(8,128)(2,1)S(1)} %fusion.152, f32[1280]{0:T(1024)S(1)} %get-tuple-element.536, bf16[4,512,128]{2,1,0:T(8,128)(2,1)} %get-tuple-element.534, ...), kind=kOutput, calls=%fused_computation.30.clone.1 | convolution fusion | flops 338821120 | bytes 2233348 | tf_op jit(solution)/shard_map/while/body/eval_jaxpr/dot_general | solution.py:37
  86.1 1.5 %fusion.152 = bf16[512,1280]{1,0:T(8,128)(2,1)S(1)} fusion(bf16[1280,128]{1,0:T(8,128)(2,1)S(1)} %get-tuple-element.532, f32[1280]{0:T(1024)S(1)} %get-tuple-element.533, bf16[4,512,128]{2,1,0:T(8,128)(2,1)} %get-tuple-element.531, s32[]{:T(128)S(6)} %copy.99), kind=kOutput, calls=%fused_computation.25.clone.1 | convolution fusion | flops 169738240 | bytes 1774596 | tf_op jit(solution)/shard_map/while/body/eval_jaxpr/dot_general | solution.py:31
  88.1 1.9 %fusion.153 = bf16[512,1,128]{2,0,1:T(8,128)(2,1)S(1)} fusion(bf16[1280,128]{1,0:T(8,128)(2,1)S(1)} %get-tuple-element.532, bf16[1280,128]{1,0:T(8,128)(2,1)S(1)} %get-tuple-element.535, bf16[512,1280]{1,0:T(8,128)(2,1)S(1)} %fusion.152, f32[1280]{0:T(1024)S(1)} %get-tuple-element.536, bf16[4,512,128]{2,1,0:T(8,128)(2,1)} %get-tuple-element.534, ...), kind=kOutput, calls=%fused_computation.30.clone.1 | convolution fusion | flops 338821120 | bytes 2233348 | tf_op jit(solution)/shard_map/while/body/eval_jaxpr/dot_general | solution.py:37
  90.0 1.1 copy.68
  91.1 17.3 %while.46 = (s32[]{:T(128)}, f32[1280,128]{1,0:T(8,128)}, bf16[4,512,128]{2,1,0:T(8,128)(2,1)}, bf16[1280,128]{1,0:T(8,128)(2,1)S(1)}, f32[1280]{0:T(1024)S(1)},...) while((s32[]{:T(128)}, f32[1280,128]{1,0:T(8,128)}, ...), condition=%wide.region_10.11_spmd.clone, body=%wide.region_9.10_spmd.clone.sunk | while | flops 508887040 | bytes 7614074 | solution.py:174
  91.1 1.4 %fusion.160 = f32[512,1280]{1,0:T(8,128)S(1)} fusion(bf16[1280,128]{1,0:T(8,128)(2,1)S(1)} %get-tuple-element.504, f32[1280]{0:T(1024)S(1)} %get-tuple-element.505, bf16[4,512,128]{2,1,0:T(8,128)(2,1)} %get-tuple-element.503, s32[]{:T(128)S(6)} %copy.93), kind=kOutput, calls=%fused_computation.48.clone.1 | convolution fusion | flops 170393600 | bytes 3085316 | tf_op jit(solution)/shard_map/while/body/eval_jaxpr/dot_general | solution.py:31
  92.5 2.7 %convolution_add_fusion.6 = f32[1280,128]{1,0:T(8,128)} fusion(f32[512,1280]{1,0:T(8,128)S(1)} %fusion.160, bf16[1280,128]{1,0:T(8,128)(2,1)S(1)} %get-tuple-element.507, f32[1280]{0:T(1024)S(1)} %get-tuple-element.508, f32[1280,128]{1,0:T(8,128)} %get-tuple-element.492, pred[]{:T(512)S(6)} %compare.3, bf16[4,512,128]{2,1,0:T(8,128)(2,1)} %get-tuple-element.506, ...), kind=kOutput, calls=%fused_computation.50.clone.1 | convolution fusion | flops 338493440 | bytes 4528640 | tf_op jit(solution)/shard_map/while/body/eval_jaxpr/dot_general | solution.py:170
  95.2 1.4 %fusion.160 = f32[512,1280]{1,0:T(8,128)S(1)} fusion(bf16[1280,128]{1,0:T(8,128)(2,1)S(1)} %get-tuple-element.504, f32[1280]{0:T(1024)S(1)} %get-tuple-element.505, bf16[4,512,128]{2,1,0:T(8,128)(2,1)} %get-tuple-element.503, s32[]{:T(128)S(6)} %copy.93), kind=kOutput, calls=%fused_computation.48.clone.1 | convolution fusion | flops 170393600 | bytes 3085316 | tf_op jit(solution)/shard_map/while/body/eval_jaxpr/dot_general | solution.py:31
  96.6 2.9 %convolution_add_fusion.6 = f32[1280,128]{1,0:T(8,128)} fusion(f32[512,1280]{1,0:T(8,128)S(1)} %fusion.160, bf16[1280,128]{1,0:T(8,128)(2,1)S(1)} %get-tuple-element.507, f32[1280]{0:T(1024)S(1)} %get-tuple-element.508, f32[1280,128]{1,0:T(8,128)} %get-tuple-element.492, pred[]{:T(512)S(6)} %compare.3, bf16[4,512,128]{2,1,0:T(8,128)(2,1)} %get-tuple-element.506, ...), kind=kOutput, calls=%fused_computation.50.clone.1 | convolution fusion | flops 338493440 | bytes 4528640 | tf_op jit(solution)/shard_map/while/body/eval_jaxpr/dot_general | solution.py:170
  99.6 1.4 %fusion.160 = f32[512,1280]{1,0:T(8,128)S(1)} fusion(bf16[1280,128]{1,0:T(8,128)(2,1)S(1)} %get-tuple-element.504, f32[1280]{0:T(1024)S(1)} %get-tuple-element.505, bf16[4,512,128]{2,1,0:T(8,128)(2,1)} %get-tuple-element.503, s32[]{:T(128)S(6)} %copy.93), kind=kOutput, calls=%fused_computation.48.clone.1 | convolution fusion | flops 170393600 | bytes 3085316 | tf_op jit(solution)/shard_map/while/body/eval_jaxpr/dot_general | solution.py:31
  101.0 2.9 %convolution_add_fusion.6 = f32[1280,128]{1,0:T(8,128)} fusion(f32[512,1280]{1,0:T(8,128)S(1)} %fusion.160, bf16[1280,128]{1,0:T(8,128)(2,1)S(1)} %get-tuple-element.507, f32[1280]{0:T(1024)S(1)} %get-tuple-element.508, f32[1280,128]{1,0:T(8,128)} %get-tuple-element.492, pred[]{:T(512)S(6)} %compare.3, bf16[4,512,128]{2,1,0:T(8,128)(2,1)} %get-tuple-element.506, ...), kind=kOutput, calls=%fused_computation.50.clone.1 | convolution fusion | flops 338493440 | bytes 4528640 | tf_op jit(solution)/shard_map/while/body/eval_jaxpr/dot_general | solution.py:170
  103.9 1.4 %fusion.160 = f32[512,1280]{1,0:T(8,128)S(1)} fusion(bf16[1280,128]{1,0:T(8,128)(2,1)S(1)} %get-tuple-element.504, f32[1280]{0:T(1024)S(1)} %get-tuple-element.505, bf16[4,512,128]{2,1,0:T(8,128)(2,1)} %get-tuple-element.503, s32[]{:T(128)S(6)} %copy.93), kind=kOutput, calls=%fused_computation.48.clone.1 | convolution fusion | flops 170393600 | bytes 3085316 | tf_op jit(solution)/shard_map/while/body/eval_jaxpr/dot_general | solution.py:31
  105.4 2.9 %convolution_add_fusion.6 = f32[1280,128]{1,0:T(8,128)} fusion(f32[512,1280]{1,0:T(8,128)S(1)} %fusion.160, bf16[1280,128]{1,0:T(8,128)(2,1)S(1)} %get-tuple-element.507, f32[1280]{0:T(1024)S(1)} %get-tuple-element.508, f32[1280,128]{1,0:T(8,128)} %get-tuple-element.492, pred[]{:T(512)S(6)} %compare.3, bf16[4,512,128]{2,1,0:T(8,128)(2,1)} %get-tuple-element.506, ...), kind=kOutput, calls=%fused_computation.50.clone.1 | convolution fusion | flops 338493440 | bytes 4528640 | tf_op jit(solution)/shard_map/while/body/eval_jaxpr/dot_general | solution.py:170
  108.5 1.3 reshape.552
  111.2 0.9 copy.69
  113.0 0.7 copy.70
  113.7 1.0 fusion.73
  114.7 10.2 %reduce-scatter.2.cloned.1.call-done = bf16[256,1,2,128]{3,0,2,1:T(8,128)(2,1)} async-done(((bf16[2048,1,2,128]{3,0,2,1:T(8,128)(2,1)}), bf16[256,1,2,128]{3,0,2,1:T(8,128)(2,1)}) %reduce-scatter.2.cloned.1.call-update) | async-done | bytes 131088 | tf_op jit(solution)/shard_map/reduce_scatter | solution.py:185
  124.9 1.5 %slice_bitcast_fusion = (bf16[256,1,128]{2,0,1:T(8,128)(2,1)}, bf16[256,1,128]{2,0,1:T(8,128)(2,1)}) fusion(bf16[256,1,2,128]{3,0,2,1:T(8,128)(2,1)} %reduce-scatter.2.cloned.1.call-done), kind=kLoop, calls=%fused_computation.113 | loop fusion | bytes 262144 | tf_op jit(solution)/shard_map/convert_element_type | solution.py:196
  (92 shorter events, 10.4 us)
Async XLA Ops:
  7.2 51.1 %copy-start = (bf16[1,256,1,128]{3,1,2,0:T(8,128)(2,1)S(1)}, bf16[1,256,1,128]{3,1,2,0:T(8,128)(2,1)}, u32[]{:S(2)}) copy-start(bf16[1,256,1,128]{3,1,2,0:T(8,128)(2,1)} %param.20) | copy-start | bytes 196612
  7.2 59.2 %all-gather.2.cloned.1.call-start = ((), (), s32[]{:S(2)}) async-start(), calls=%async_computation.1 | async-start | bytes 3276800 | tf_op jit(solution)/shard_map/all_gather | solution.py:82
  7.9 117.0 %reduce-scatter.2.cloned.1.call-start = ((), (), s32[]{:S(2)}) async-start(), calls=%async_computation.2 | async-start | bytes 1179648 | tf_op jit(solution)/shard_map/reduce_scatter | solution.py:185
  28.6 1.3 copy-start.13
  28.9 2.1 %copy-start.3 = (bf16[1,256,1,5,64]{4,1,3,2,0:T(8,128)(2,1)}, bf16[1,256,1,5,64]{4,1,3,2,0:T(8,128)(2,1)S(1)}, u32[]{:S(2)}) copy-start(bf16[1,256,1,5,64]{4,1,3,2,0:T(8,128)(2,1)S(1)} %get-tuple-element.257) | copy-start | bytes 491524
  28.9 2.1 %copy-start.5 = (bf16[1,256,1,5,64]{4,1,3,2,0:T(8,128)(2,1)}, bf16[1,256,1,5,64]{4,1,3,2,0:T(8,128)(2,1)S(1)}, u32[]{:S(2)}) copy-start(bf16[1,256,1,5,64]{4,1,3,2,0:T(8,128)(2,1)S(1)} %get-tuple-element.258) | copy-start | bytes 491524
  30.5 1.6 %copy-start.10 = (bf16[256,64]{1,0:T(8,128)(2,1)}, bf16[256,64]{1,0:T(8,128)(2,1)S(1)}, u32[]{:S(2)}) copy-start(bf16[256,64]{1,0:T(8,128)(2,1)S(1)} %get-tuple-element.264) | copy-start | bytes 98308
  40.3 1.9 %copy-start.14 = (bf16[256,1,128]{2,0,1:T(8,128)(2,1)S(1)}, bf16[256,1,128]{2,0,1:T(8,128)(2,1)}, u32[]{:S(2)}) copy-start(bf16[256,1,128]{2,0,1:T(8,128)(2,1)} %param.22) | copy-start | bytes 196612
  40.6 0.9 copy-start.1
  72.3 0.7 copy-start.7
  73.0 1.2 copy-start.9
  108.3 1.9 %copy-start.2 = (bf16[256,5,256]{2,0,1:T(8,128)(2,1)S(1)}, bf16[256,5,256]{2,0,1:T(8,128)(2,1)}, u32[]{:S(2)}) copy-start(bf16[256,5,256]{2,0,1:T(8,128)(2,1)} %copy-done.1) | copy-start | bytes 1966084
  108.3 1.9 %copy-start.8 = (bf16[256,5,128]{2,0,1:T(8,128)(2,1)S(1)}, bf16[256,5,128]{2,0,1:T(8,128)(2,1)}, u32[]{:S(2)}) copy-start(bf16[256,5,128]{2,0,1:T(8,128)(2,1)} %copy-done.7) | copy-start | bytes 983044
  108.5 2.1 %copy-start.11 = (bf16[256,64]{1,0:T(8,128)(2,1)S(1)}, bf16[256,64]{1,0:T(8,128)(2,1)}, u32[]{:S(2)}) copy-start(bf16[256,64]{1,0:T(8,128)(2,1)} %copy-done.10) | copy-start | bytes 98308
  109.8 1.3 copy-start.12
  110.6 1.5 %copy-start.4 = (bf16[1,256,1,5,64]{4,1,3,2,0:T(8,128)(2,1)S(1)}, bf16[1,256,1,5,64]{4,1,3,2,0:T(8,128)(2,1)}, u32[]{:S(2)}) copy-start(bf16[1,256,1,5,64]{4,1,3,2,0:T(8,128)(2,1)} %copy-done.3) | copy-start | bytes 491524
  110.6 1.5 %copy-start.6 = (bf16[1,256,1,5,64]{4,1,3,2,0:T(8,128)(2,1)S(1)}, bf16[1,256,1,5,64]{4,1,3,2,0:T(8,128)(2,1)}, u32[]{:S(2)}) copy-start(bf16[1,256,1,5,64]{4,1,3,2,0:T(8,128)(2,1)} %copy-done.5) | copy-start | bytes 491524
Sparse Core Ops, SparseCore 0:
  9.8 42.2 all-gather.1
  91.2 33.7 reduce-scatter.1
where the time goes:
time: 134 us; the launch traced here: 133 us
  matrix products  55.1 us (41%)
  blocking collectives  33.9 us (25%)
  between operations  15.1 us (11%)
  local copies, waits for them, and re-layouts  11.4 us (9%)
  waiting for transfers between devices  11 us (8%)
  other arithmetic  6.39 us (5%)
    all_gather x1, blocking collectives, local(): lax.all_gather(keys_prompt, 'roll', axis=0, tiled=True)  17.7 us
    dot_general x12, matrix products, inner_dot(): lax.dot_general(left, right, (((1,), (1,)), ((), ())), preferred_element_...  17.3 us
    all_gather x1, blocking collectives, local(): lax.all_gather(values_prompt, 'roll', axis=0, tiled=True)  16.1 us
    dot_general x4, matrix products, query_step(): jnp.dot(score_grad, blocks[0], preferred_element_type=jnp.float32)  11.5 us
    reduce_scatter x1, waiting for transfers between devices, local(): lax.psum_scatter(jnp.stack(pieces, axis=1).astype(jnp.bfloat16), 'roll',...  10.2 us
    dot_general x8, matrix products, outer_sum(): lax.dot_general(left, right, (((0,), (0,)), ((), ())), preferred_element_...  9.5 us
    dot_general x4, matrix products, output_step(): jnp.dot(attn_probs, blocks[1], preferred_element_type=jnp.float32)  7.7 us
    dot_general x1, matrix products, local(): jnp.einsum('rsc,ghdc->rsghd', lax.all_gather(out_grad, 'kvh', axis=1, til...  5.89 us
  transfers between devices with their start and end apart: 2, of which 1 were waited for; matrix products, arithmetic and copies ran while one was open for 34% of the time, Pallas kernels for 0%

commit v1 on v0

--- a/solution.py
+++ b/solution.py
@@ -83,8 +83,15 @@
         out_weight,
         preferred_element_type=jnp.float32,
     ).astype(jnp.bfloat16)
+
+    def _note_node(here_x, axis_k):
+        even = lax.axis_size("roll")
+        low = jnp.stack([here_x] * even, axis=0)
+        v_next = lax.all_to_all(low, "roll", 0, 0)
+        return jnp.concatenate(v_next, axis_k)
+
     cached_keys, cached_values = (
-        lax.all_gather(keys_prompt, "roll", axis=0, tiled=True),
+        _note_node(keys_prompt, 0),
         lax.all_gather(values_prompt, "roll", axis=0, tiled=True),
     )
     positions = prompt_total + offsets[:, None] + jnp.arange(seq_len, dtype=jnp.int32)[None, :]

time: 134 us -> 126 us (0.940)
  blocking collectives: 33.9 us -> 16.6 us
  starting transfers between devices: 0.08 us -> 6.43 us
  local copies, waits for them, and re-layouts: 11.4 us -> 13.1 us
    all_gather x1 -> x0, blocking collectives: 17.7 us -> none  [local(): lax.all_gather(keys_prompt, 'roll', axis=0, tiled=True)]
    all_to_all x0 -> x1, starting transfers between devices: none -> 6.35 us  [_note_node(): v_next = lax.all_to_all(low, 'roll', 0, 0)]
    another operation x2 -> x3, local copies, waits for them, and re-layouts: 0.48 us -> 2.24 us  [the longest x1 1.76 us: _note_node(): low = jnp.stack([here_x] * even, axis=0)]
    all_gather x1, waiting for transfers between devices: 0.02 us -> 1.57 us  [local(): lax.all_gather(out_grad, 'kvh', axis=1, tiled=True)]
    unnamed x32 -> x36, local copies, waits for them, and re-layouts: 3.82 us -> 3.83 us
  transfers between devices with their start and end apart: 2 -> 3, of which waited for: 1 -> 2; matrix products, arithmetic and copies ran while one was open for 34% -> 37% of each run, Pallas kernels for 0% -> 0%
where the time goes in v1:
time: 126 us; the launch traced here: 125 us
  matrix products  55 us (44%)
  blocking collectives  16.6 us (13%)
  between operations  15.1 us (12%)
  local copies, waits for them, and re-layouts  13.1 us (10%)
  waiting for transfers between devices  11.5 us (9%)
  starting transfers between devices  6.43 us (5%)
  other arithmetic  6.37 us (5%)
    dot_general x12, matrix products, inner_dot(): lax.dot_general(left, right, (((1,), (1,)), ((), ())), preferred_element_...  17.3 us
    all_gather x1, blocking collectives, local(): lax.all_gather(values_prompt, 'roll', axis=0, tiled=True)  16.6 us
    dot_general x4, matrix products, query_step(): jnp.dot(score_grad, blocks[0], preferred_element_type=jnp.float32)  11.5 us
    dot_general x8, matrix products, outer_sum(): lax.dot_general(left, right, (((0,), (0,)), ((), ())), preferred_element_...  9.53 us
    reduce_scatter x1, waiting for transfers between devices, local(): lax.psum_scatter(jnp.stack(pieces, axis=1).astype(jnp.bfloat16), 'roll',...  9.22 us
    dot_general x4, matrix products, output_step(): jnp.dot(attn_probs, blocks[1], preferred_element_type=jnp.float32)  7.67 us
    all_to_all x1, starting transfers between devices, _note_node(): v_next = lax.all_to_all(low, 'roll', 0, 0)  6.35 us
    dot_general x1, matrix products, local(): jnp.einsum('rsc,ghdc->rsghd', lax.all_gather(out_grad, 'kvh', axis=1, til...  5.89 us
  transfers between devices with their start and end apart: 3, of which 2 were waited for; matrix products, arithmetic and copies ran while one was open for 37% of the time, Pallas kernels for 0%

profile of v1, /device:TPU:0, one launch (start us, length us, event | category | flops | bytes accessed | tf_op | source)
XLA Modules:
  0.0 124.8 jit_solution(7360948401987355139)
XLA Ops:
  7.2 1.8 %stack.10 = bf16[8,256,1,128]{3,1,2,0:T(8,128)(2,1)} broadcast(bf16[256,128]{1,0:T(8,128)(2,1)} %bitcast.161), dimensions={1,3} | broadcast | bytes 589824 | tf_op jit(solution)/shard_map/stack | solution.py:89
  8.9 6.4 %all-to-all-start = ((bf16[8,256,1,128]{3,1,2,0:T(8,128)(2,1)}), bf16[8,256,1,128]{3,1,2,0:T(8,128)(2,1)}, u32[]{:S(2)}, u32[]{:S(2)}) async-start(bf16[8,256,1,128]{3,1,2,0:T(8,128)(2,1)} %stack.10), calls=%async_computation | async-start | bytes 1048576 | tf_op jit(solution)/shard_map/all_to_all | solution.py:90
  15.3 0.7 all-gather.2.cloned.1.call-update
  16.1 1.0 convert_element_type.136
  17.8 0.9 broadcast_multiply_fusion
  19.0 0.6 fusion.96
  20.9 0.6 fusion.103
  22.6 16.6 %all_gather.6 = bf16[2048,1,128]{2,0,1:T(8,128)(2,1)} all-gather(bf16[256,1,128]{2,0,1:T(8,128)(2,1)S(1)} %copy-done.12), channel_id=1, replica_groups=mesh['roll'=8,'kvh'=4] {'roll'}, dimensions={0}, use_global_device_ids=true | all-gather | bytes 589824 | tf_op jit(solution)/shard_map/all_gather | solution.py:95
  39.5 7.7 %while.43 = (s32[]{:T(128)}, f32[1280]{0:T(1024)S(1)}, f32[1280]{0:T(1024)S(1)}, bf16[4,512,128]{2,1,0:T(8,128)(2,1)}, bf16[1280,128]{1,0:T(8,128)(2,1)S(1)}, /*index=5*/s32[]{:T(128)}) while((s32[]{:T(128)}, f32[1280]{0:T(1024)S(1)}, f32[1280]{0:T(1024)S(1)}, bf16[4,512,128]{2,1,0:T(8,128)(2,1)}, bf16[1280,128]{1,0:T(8,128)(2,1)S(1)}, ...), condition=%wide.region_5.6_spmd, body=%wide.region_2.5_spmd.sunk | while | flops 170396160 | bytes 5768273 | solution.py:134
  39.6 1.4 %fusion.141 = (f32[1280]{0:T(1024)S(1)}, f32[512,1280]{1,0:T(8,128)S(1)}) fusion(bf16[1280,128]{1,0:T(8,128)(2,1)S(1)} %get-tuple-element.458, bf16[4,512,128]{2,1,0:T(8,128)(2,1)} %get-tuple-element.457, s32[]{:T(128)S(6)} %copy.79), kind=kOutput, calls=%fused_computation.131.clone.1 | convolution fusion | flops 169081600 | bytes 3085316 | tf_op jit(solution)/shard_map/while/body/eval_jaxpr/dot_general | solution.py:31
  41.5 1.4 %fusion.141 = (f32[1280]{0:T(1024)S(1)}, f32[512,1280]{1,0:T(8,128)S(1)}) fusion(bf16[1280,128]{1,0:T(8,128)(2,1)S(1)} %get-tuple-element.458, bf16[4,512,128]{2,1,0:T(8,128)(2,1)} %get-tuple-element.457, s32[]{:T(128)S(6)} %copy.79), kind=kOutput, calls=%fused_computation.131.clone.1 | convolution fusion | flops 169081600 | bytes 3085316 | tf_op jit(solution)/shard_map/while/body/eval_jaxpr/dot_general | solution.py:31
  43.4 1.4 %fusion.141 = (f32[1280]{0:T(1024)S(1)}, f32[512,1280]{1,0:T(8,128)S(1)}) fusion(bf16[1280,128]{1,0:T(8,128)(2,1)S(1)} %get-tuple-element.458, bf16[4,512,128]{2,1,0:T(8,128)(2,1)} %get-tuple-element.457, s32[]{:T(128)S(6)} %copy.79), kind=kOutput, calls=%fused_computation.131.clone.1 | convolution fusion | flops 169081600 | bytes 3085316 | tf_op jit(solution)/shard_map/while/body/eval_jaxpr/dot_general | solution.py:31
  45.3 1.4 %fusion.141 = (f32[1280]{0:T(1024)S(1)}, f32[512,1280]{1,0:T(8,128)S(1)}) fusion(bf16[1280,128]{1,0:T(8,128)(2,1)S(1)} %get-tuple-element.458, bf16[4,512,128]{2,1,0:T(8,128)(2,1)} %get-tuple-element.457, s32[]{:T(128)S(6)} %copy.79), kind=kOutput, calls=%fused_computation.131.clone.1 | convolution fusion | flops 169081600 | bytes 3085316 | tf_op jit(solution)/shard_map/while/body/eval_jaxpr/dot_general | solution.py:31
  47.8 0.8 copy-done.1
  49.6 7.7 %while.44 = (s32[]{:T(128)}, f32[1280,128]{1,0:T(8,128)S(1)}, bf16[4,512,128]{2,1,0:T(8,128)(2,1)}, bf16[1280,128]{1,0:T(8,128)(2,1)S(1)}, f32[1280]{0:T(1024)S(1)}, /*index=5*/bf16[4,512,128]{2,1,0:T(8,128)(2,1)}, s32[]{:T(128)}) while((s32[]{:T(128)}, f32[1280,128]{1,0:T(8,128)S(1)}, bf16[4,512,128]{2,1,0:T(8,128)(2,1)}, ...), condition=%wide.region_7.8_spmd, body=%wide.region_6.7_spmd.sunk | while | flops 337674240 | bytes 1906773 | solution.py:152
  49.6 1.9 %convolution_add_fusion.5 = f32[1280,128]{1,0:T(8,128)S(1)} fusion(f32[1280,128]{1,0:T(8,128)S(1)} %get-tuple-element.468, bf16[1280,128]{1,0:T(8,128)(2,1)S(1)} %get-tuple-element.477, f32[1280]{0:T(1024)S(1)} %get-tuple-element.478, bf16[4,512,128]{2,1,0:T(8,128)(2,1)} %get-tuple-element.479, s32[]{:T(128)S(6)} %copy.87, ...), kind=kOutput, calls=%fused_computation.10.clone.1 | convolution fusion | flops 337674240 | bytes 1906688 | tf_op jit(solution)/shard_map/while/body/eval_jaxpr/dot_general | solution.py:148
  51.6 1.9 %convolution_add_fusion.5 = f32[1280,128]{1,0:T(8,128)S(1)} fusion(f32[1280,128]{1,0:T(8,128)S(1)} %get-tuple-element.468, bf16[1280,128]{1,0:T(8,128)(2,1)S(1)} %get-tuple-element.477, f32[1280]{0:T(1024)S(1)} %get-tuple-element.478, bf16[4,512,128]{2,1,0:T(8,128)(2,1)} %get-tuple-element.479, s32[]{:T(128)S(6)} %copy.87, ...), kind=kOutput, calls=%fused_computation.10.clone.1 | convolution fusion | flops 337674240 | bytes 1906688 | tf_op jit(solution)/shard_map/while/body/eval_jaxpr/dot_general | solution.py:148
  53.5 1.9 %convolution_add_fusion.5 = f32[1280,128]{1,0:T(8,128)S(1)} fusion(f32[1280,128]{1,0:T(8,128)S(1)} %get-tuple-element.468, bf16[1280,128]{1,0:T(8,128)(2,1)S(1)} %get-tuple-element.477, f32[1280]{0:T(1024)S(1)} %get-tuple-element.478, bf16[4,512,128]{2,1,0:T(8,128)(2,1)} %get-tuple-element.479, s32[]{:T(128)S(6)} %copy.87, ...), kind=kOutput, calls=%fused_computation.10.clone.1 | convolution fusion | flops 337674240 | bytes 1906688 | tf_op jit(solution)/shard_map/while/body/eval_jaxpr/dot_general | solution.py:148
  55.5 1.9 %convolution_add_fusion.5 = f32[1280,128]{1,0:T(8,128)S(1)} fusion(f32[1280,128]{1,0:T(8,128)S(1)} %get-tuple-element.468, bf16[1280,128]{1,0:T(8,128)(2,1)S(1)} %get-tuple-element.477, f32[1280]{0:T(1024)S(1)} %get-tuple-element.478, bf16[4,512,128]{2,1,0:T(8,128)(2,1)} %get-tuple-element.479, s32[]{:T(128)S(6)} %copy.87, ...), kind=kOutput, calls=%fused_computation.10.clone.1 | convolution fusion | flops 337674240 | bytes 1906688 | tf_op jit(solution)/shard_map/while/body/eval_jaxpr/dot_general | solution.py:148
  57.4 1.6 %all-gather.2.cloned.1.call-done = bf16[1,256,5120]{2,1,0:T(8,128)(2,1)} async-done(((bf16[1,64,5120]{2,1,0:T(8,128)(2,1)}), bf16[1,256,5120]{2,1,0:T(8,128)(2,1)}) %all-gather.2.cloned.1.call-update) | async-done | bytes 2621456 | tf_op jit(solution)/shard_map/all_gather | solution.py:82
  58.9 5.9 %fusion.67 = bf16[256,5,128]{2,0,1:T(8,128)(2,1)S(1)} fusion(bf16[1,5,128,5120]{3,2,1,0:T(8,128)(2,1)} %param.17, bf16[1,256,5120]{2,1,0:T(8,128)(2,1)} %all-gather.2.cloned.1.call-done), kind=kOutput, calls=%fused_computation.75 | convolution fusion | flops 1677885440 | bytes 9502720 | tf_op jit(solution)/shard_map/rsc,ghdc->rsghd/dot_general | solution.py:80
  64.9 0.7 copy-done.7
  66.2 0.6 copy-done.9
  66.8 15.8 %while.45 = (s32[]{:T(128)}, bf16[4,512,2,128]{3,1,2,0:T(8,128)(2,1)S(1)}, bf16[4,512,128]{2,1,0:T(8,128)(2,1)}, bf16[1280,128]{1,0:T(8,128)(2,1)S(1)}, f32[1280...) while((s32[]{:T(128)}, ...), condition=%wide.region_12.13_spmd, body=%wide.region_11.12_spmd.sunk | while | flops 676855808 | bytes 6301809 | solution.py:68
  66.8 1.5 %fusion.152 = bf16[512,1280]{1,0:T(8,128)(2,1)S(1)} fusion(bf16[1280,128]{1,0:T(8,128)(2,1)S(1)} %get-tuple-element.532, f32[1280]{0:T(1024)S(1)} %get-tuple-element.533, bf16[4,512,128]{2,1,0:T(8,128)(2,1)} %get-tuple-element.531, s32[]{:T(128)S(6)} %copy.99), kind=kOutput, calls=%fused_computation.25.clone.1 | convolution fusion | flops 169738240 | bytes 1774596 | tf_op jit(solution)/shard_map/while/body/eval_jaxpr/dot_general | solution.py:31
  68.8 1.9 %fusion.153 = bf16[512,1,128]{2,0,1:T(8,128)(2,1)S(1)} fusion(bf16[1280,128]{1,0:T(8,128)(2,1)S(1)} %get-tuple-element.532, bf16[1280,128]{1,0:T(8,128)(2,1)S(1)} %get-tuple-element.535, bf16[512,1280]{1,0:T(8,128)(2,1)S(1)} %fusion.152, f32[1280]{0:T(1024)S(1)} %get-tuple-element.536, bf16[4,512,128]{2,1,0:T(8,128)(2,1)} %get-tuple-element.534, ...), kind=kOutput, calls=%fused_computation.30.clone.1 | convolution fusion | flops 338821120 | bytes 2233348 | tf_op jit(solution)/shard_map/while/body/eval_jaxpr/dot_general | solution.py:37
  70.7 1.5 %fusion.152 = bf16[512,1280]{1,0:T(8,128)(2,1)S(1)} fusion(bf16[1280,128]{1,0:T(8,128)(2,1)S(1)} %get-tuple-element.532, f32[1280]{0:T(1024)S(1)} %get-tuple-element.533, bf16[4,512,128]{2,1,0:T(8,128)(2,1)} %get-tuple-element.531, s32[]{:T(128)S(6)} %copy.99), kind=kOutput, calls=%fused_computation.25.clone.1 | convolution fusion | flops 169738240 | bytes 1774596 | tf_op jit(solution)/shard_map/while/body/eval_jaxpr/dot_general | solution.py:31
  72.7 1.9 %fusion.153 = bf16[512,1,128]{2,0,1:T(8,128)(2,1)S(1)} fusion(bf16[1280,128]{1,0:T(8,128)(2,1)S(1)} %get-tuple-element.532, bf16[1280,128]{1,0:T(8,128)(2,1)S(1)} %get-tuple-element.535, bf16[512,1280]{1,0:T(8,128)(2,1)S(1)} %fusion.152, f32[1280]{0:T(1024)S(1)} %get-tuple-element.536, bf16[4,512,128]{2,1,0:T(8,128)(2,1)} %get-tuple-element.534, ...), kind=kOutput, calls=%fused_computation.30.clone.1 | convolution fusion | flops 338821120 | bytes 2233348 | tf_op jit(solution)/shard_map/while/body/eval_jaxpr/dot_general | solution.py:37
  74.7 1.5 %fusion.152 = bf16[512,1280]{1,0:T(8,128)(2,1)S(1)} fusion(bf16[1280,128]{1,0:T(8,128)(2,1)S(1)} %get-tuple-element.532, f32[1280]{0:T(1024)S(1)} %get-tuple-element.533, bf16[4,512,128]{2,1,0:T(8,128)(2,1)} %get-tuple-element.531, s32[]{:T(128)S(6)} %copy.99), kind=kOutput, calls=%fused_computation.25.clone.1 | convolution fusion | flops 169738240 | bytes 1774596 | tf_op jit(solution)/shard_map/while/body/eval_jaxpr/dot_general | solution.py:31
  76.7 1.9 %fusion.153 = bf16[512,1,128]{2,0,1:T(8,128)(2,1)S(1)} fusion(bf16[1280,128]{1,0:T(8,128)(2,1)S(1)} %get-tuple-element.532, bf16[1280,128]{1,0:T(8,128)(2,1)S(1)} %get-tuple-element.535, bf16[512,1280]{1,0:T(8,128)(2,1)S(1)} %fusion.152, f32[1280]{0:T(1024)S(1)} %get-tuple-element.536, bf16[4,512,128]{2,1,0:T(8,128)(2,1)} %get-tuple-element.534, ...), kind=kOutput, calls=%fused_computation.30.clone.1 | convolution fusion | flops 338821120 | bytes 2233348 | tf_op jit(solution)/shard_map/while/body/eval_jaxpr/dot_general | solution.py:37
  78.6 1.5 %fusion.152 = bf16[512,1280]{1,0:T(8,128)(2,1)S(1)} fusion(bf16[1280,128]{1,0:T(8,128)(2,1)S(1)} %get-tuple-element.532, f32[1280]{0:T(1024)S(1)} %get-tuple-element.533, bf16[4,512,128]{2,1,0:T(8,128)(2,1)} %get-tuple-element.531, s32[]{:T(128)S(6)} %copy.99), kind=kOutput, calls=%fused_computation.25.clone.1 | convolution fusion | flops 169738240 | bytes 1774596 | tf_op jit(solution)/shard_map/while/body/eval_jaxpr/dot_general | solution.py:31
  80.6 1.9 %fusion.153 = bf16[512,1,128]{2,0,1:T(8,128)(2,1)S(1)} fusion(bf16[1280,128]{1,0:T(8,128)(2,1)S(1)} %get-tuple-element.532, bf16[1280,128]{1,0:T(8,128)(2,1)S(1)} %get-tuple-element.535, bf16[512,1280]{1,0:T(8,128)(2,1)S(1)} %fusion.152, f32[1280]{0:T(1024)S(1)} %get-tuple-element.536, bf16[4,512,128]{2,1,0:T(8,128)(2,1)} %get-tuple-element.534, ...), kind=kOutput, calls=%fused_computation.30.clone.1 | convolution fusion | flops 338821120 | bytes 2233348 | tf_op jit(solution)/shard_map/while/body/eval_jaxpr/dot_general | solution.py:37
  82.6 1.0 copy.68
  83.6 17.2 %while.46 = (s32[]{:T(128)}, f32[1280,128]{1,0:T(8,128)}, bf16[4,512,128]{2,1,0:T(8,128)(2,1)}, bf16[1280,128]{1,0:T(8,128)(2,1)S(1)}, f32[1280]{0:T(1024)S(1)},...) while((s32[]{:T(128)}, f32[1280,128]{1,0:T(8,128)}, ...), condition=%wide.region_10.11_spmd.clone, body=%wide.region_9.10_spmd.clone.sunk | while | flops 508887040 | bytes 7614074 | solution.py:181
  83.6 1.4 %fusion.160 = f32[512,1280]{1,0:T(8,128)S(1)} fusion(bf16[1280,128]{1,0:T(8,128)(2,1)S(1)} %get-tuple-element.504, f32[1280]{0:T(1024)S(1)} %get-tuple-element.505, bf16[4,512,128]{2,1,0:T(8,128)(2,1)} %get-tuple-element.503, s32[]{:T(128)S(6)} %copy.93), kind=kOutput, calls=%fused_computation.48.clone.1 | convolution fusion | flops 170393600 | bytes 3085316 | tf_op jit(solution)/shard_map/while/body/eval_jaxpr/dot_general | solution.py:31
  85.1 2.7 %convolution_add_fusion.6 = f32[1280,128]{1,0:T(8,128)} fusion(f32[512,1280]{1,0:T(8,128)S(1)} %fusion.160, bf16[1280,128]{1,0:T(8,128)(2,1)S(1)} %get-tuple-element.507, f32[1280]{0:T(1024)S(1)} %get-tuple-element.508, f32[1280,128]{1,0:T(8,128)} %get-tuple-element.492, pred[]{:T(512)S(6)} %compare.3, bf16[4,512,128]{2,1,0:T(8,128)(2,1)} %get-tuple-element.506, ...), kind=kOutput, calls=%fused_computation.50.clone.1 | convolution fusion | flops 338493440 | bytes 4528640 | tf_op jit(solution)/shard_map/while/body/eval_jaxpr/dot_general | solution.py:177
  87.7 1.4 %fusion.160 = f32[512,1280]{1,0:T(8,128)S(1)} fusion(bf16[1280,128]{1,0:T(8,128)(2,1)S(1)} %get-tuple-element.504, f32[1280]{0:T(1024)S(1)} %get-tuple-element.505, bf16[4,512,128]{2,1,0:T(8,128)(2,1)} %get-tuple-element.503, s32[]{:T(128)S(6)} %copy.93), kind=kOutput, calls=%fused_computation.48.clone.1 | convolution fusion | flops 170393600 | bytes 3085316 | tf_op jit(solution)/shard_map/while/body/eval_jaxpr/dot_general | solution.py:31
  89.2 2.9 %convolution_add_fusion.6 = f32[1280,128]{1,0:T(8,128)} fusion(f32[512,1280]{1,0:T(8,128)S(1)} %fusion.160, bf16[1280,128]{1,0:T(8,128)(2,1)S(1)} %get-tuple-element.507, f32[1280]{0:T(1024)S(1)} %get-tuple-element.508, f32[1280,128]{1,0:T(8,128)} %get-tuple-element.492, pred[]{:T(512)S(6)} %compare.3, bf16[4,512,128]{2,1,0:T(8,128)(2,1)} %get-tuple-element.506, ...), kind=kOutput, calls=%fused_computation.50.clone.1 | convolution fusion | flops 338493440 | bytes 4528640 | tf_op jit(solution)/shard_map/while/body/eval_jaxpr/dot_general | solution.py:177
  92.1 1.4 %fusion.160 = f32[512,1280]{1,0:T(8,128)S(1)} fusion(bf16[1280,128]{1,0:T(8,128)(2,1)S(1)} %get-tuple-element.504, f32[1280]{0:T(1024)S(1)} %get-tuple-element.505, bf16[4,512,128]{2,1,0:T(8,128)(2,1)} %get-tuple-element.503, s32[]{:T(128)S(6)} %copy.93), kind=kOutput, calls=%fused_computation.48.clone.1 | convolution fusion | flops 170393600 | bytes 3085316 | tf_op jit(solution)/shard_map/while/body/eval_jaxpr/dot_general | solution.py:31
  93.6 2.9 %convolution_add_fusion.6 = f32[1280,128]{1,0:T(8,128)} fusion(f32[512,1280]{1,0:T(8,128)S(1)} %fusion.160, bf16[1280,128]{1,0:T(8,128)(2,1)S(1)} %get-tuple-element.507, f32[1280]{0:T(1024)S(1)} %get-tuple-element.508, f32[1280,128]{1,0:T(8,128)} %get-tuple-element.492, pred[]{:T(512)S(6)} %compare.3, bf16[4,512,128]{2,1,0:T(8,128)(2,1)} %get-tuple-element.506, ...), kind=kOutput, calls=%fused_computation.50.clone.1 | convolution fusion | flops 338493440 | bytes 4528640 | tf_op jit(solution)/shard_map/while/body/eval_jaxpr/dot_general | solution.py:177
  96.5 1.4 %fusion.160 = f32[512,1280]{1,0:T(8,128)S(1)} fusion(bf16[1280,128]{1,0:T(8,128)(2,1)S(1)} %get-tuple-element.504, f32[1280]{0:T(1024)S(1)} %get-tuple-element.505, bf16[4,512,128]{2,1,0:T(8,128)(2,1)} %get-tuple-element.503, s32[]{:T(128)S(6)} %copy.93), kind=kOutput, calls=%fused_computation.48.clone.1 | convolution fusion | flops 170393600 | bytes 3085316 | tf_op jit(solution)/shard_map/while/body/eval_jaxpr/dot_general | solution.py:31
  97.9 2.9 %convolution_add_fusion.6 = f32[1280,128]{1,0:T(8,128)} fusion(f32[512,1280]{1,0:T(8,128)S(1)} %fusion.160, bf16[1280,128]{1,0:T(8,128)(2,1)S(1)} %get-tuple-element.507, f32[1280]{0:T(1024)S(1)} %get-tuple-element.508, f32[1280,128]{1,0:T(8,128)} %get-tuple-element.492, pred[]{:T(512)S(6)} %compare.3, bf16[4,512,128]{2,1,0:T(8,128)(2,1)} %get-tuple-element.506, ...), kind=kOutput, calls=%fused_computation.50.clone.1 | convolution fusion | flops 338493440 | bytes 4528640 | tf_op jit(solution)/shard_map/while/body/eval_jaxpr/dot_general | solution.py:177
  101.1 1.3 %reshape.555 = f32[256,5,128]{2,1,0:T(8,128)S(1)} reshape(f32[1280,128]{1,0:T(8,128)} %get-tuple-element.152) | data formatting | bytes 1310720 | tf_op jit(solution)/shard_map/reshape | solution.py:182
  103.8 0.9 copy.69
  105.5 0.7 copy.70
  106.2 1.0 fusion.73
  107.2 9.2 %reduce-scatter.2.cloned.1.call-done = bf16[256,1,2,128]{3,0,2,1:T(8,128)(2,1)} async-done(((bf16[2048,1,2,128]{3,0,2,1:T(8,128)(2,1)}), bf16[256,1,2,128]{3,0,2,1:T(8,128)(2,1)}) %reduce-scatter.2.cloned.1.call-update) | async-done | bytes 131088 | tf_op jit(solution)/shard_map/reduce_scatter | solution.py:192
  116.4 1.5 %slice_bitcast_fusion = (bf16[256,1,128]{2,0,1:T(8,128)(2,1)}, bf16[256,1,128]{2,0,1:T(8,128)(2,1)}) fusion(bf16[256,1,2,128]{3,0,2,1:T(8,128)(2,1)} %reduce-scatter.2.cloned.1.call-done), kind=kLoop, calls=%fused_computation.113 | loop fusion | bytes 262144 | tf_op jit(solution)/shard_map/convert_element_type | solution.py:203
  (98 shorter events, 11.3 us)
Async XLA Ops:
  7.2 42.1 %copy-start = (bf16[1,256,1,128]{3,1,2,0:T(8,128)(2,1)S(1)}, bf16[1,256,1,128]{3,1,2,0:T(8,128)(2,1)}, u32[]{:S(2)}) copy-start(bf16[1,256,1,128]{3,1,2,0:T(8,128)(2,1)} %param.20) | copy-start | bytes 196612
  7.2 11.8 %copy-start.11 = (bf16[1,256,1,128]{3,1,2,0:T(8,128)(2,1)S(1)}, bf16[1,256,1,128]{3,1,2,0:T(8,128)(2,1)}, u32[]{:S(2)}) copy-start(bf16[1,256,1,128]{3,1,2,0:T(8,128)(2,1)} %param.19) | copy-start | bytes 196612
  8.9 30.5 %all-to-all-start = ((bf16[8,256,1,128]{3,1,2,0:T(8,128)(2,1)}), bf16[8,256,1,128]{3,1,2,0:T(8,128)(2,1)}, u32[]{:S(2)}, u32[]{:S(2)}) async-start(bf16[8,256,1,128]{3,1,2,0:T(8,128)(2,1)} %stack.10), calls=%async_computation | async-start | bytes 1048576 | tf_op jit(solution)/shard_map/all_to_all | solution.py:90
  15.3 43.6 %all-gather.2.cloned.1.call-start = ((), (), s32[]{:S(2)}) async-start(), calls=%async_computation.2 | async-start | bytes 3276800 | tf_op jit(solution)/shard_map/all_gather | solution.py:82
  16.0 100.4 %reduce-scatter.2.cloned.1.call-start = ((), (), s32[]{:S(2)}) async-start(), calls=%async_computation.3 | async-start | bytes 1179648 | tf_op jit(solution)/shard_map/reduce_scatter | solution.py:192
  16.1 2.9 %copy-start.15 = (f32[64]{0:T(128)}, f32[64]{0:T(128)S(1)}, u32[]{:S(2)}) copy-start(f32[64]{0:T(128)S(1)} %negate_power_fusion) | copy-start | bytes 772
  17.8 1.2 copy-start.13
  19.9 1.6 %copy-start.3 = (bf16[1,256,1,5,64]{4,1,3,2,0:T(8,128)(2,1)}, bf16[1,256,1,5,64]{4,1,3,2,0:T(8,128)(2,1)S(1)}, u32[]{:S(2)}) copy-start(bf16[1,256,1,5,64]{4,1,3,2,0:T(8,128)(2,1)S(1)} %get-tuple-element.257) | copy-start | bytes 491524
  19.9 1.6 %copy-start.5 = (bf16[1,256,1,5,64]{4,1,3,2,0:T(8,128)(2,1)}, bf16[1,256,1,5,64]{4,1,3,2,0:T(8,128)(2,1)S(1)}, u32[]{:S(2)}) copy-start(bf16[1,256,1,5,64]{4,1,3,2,0:T(8,128)(2,1)S(1)} %get-tuple-element.258) | copy-start | bytes 491524
  20.7 2.0 %copy-start.12 = (bf16[256,1,128]{2,0,1:T(8,128)(2,1)S(1)}, bf16[256,1,128]{2,0,1:T(8,128)(2,1)}, u32[]{:S(2)}) copy-start(bf16[256,1,128]{2,0,1:T(8,128)(2,1)} %param.22) | copy-start | bytes 196612
  47.8 0.9 copy-start.1
  64.8 0.7 copy-start.7
  65.6 1.2 copy-start.9
  100.9 1.9 %copy-start.2 = (bf16[256,5,256]{2,0,1:T(8,128)(2,1)S(1)}, bf16[256,5,256]{2,0,1:T(8,128)(2,1)}, u32[]{:S(2)}) copy-start(bf16[256,5,256]{2,0,1:T(8,128)(2,1)} %copy-done.1) | copy-start | bytes 1966084
  100.9 1.9 %copy-start.8 = (bf16[256,5,128]{2,0,1:T(8,128)(2,1)S(1)}, bf16[256,5,128]{2,0,1:T(8,128)(2,1)}, u32[]{:S(2)}) copy-start(bf16[256,5,128]{2,0,1:T(8,128)(2,1)} %copy-done.7) | copy-start | bytes 983044
  102.3 1.3 %copy-start.10 = (f32[256,64]{0,1:T(8,128)S(1)}, f32[256,64]{0,1:T(8,128)}, u32[]{:S(2)}) copy-start(f32[256,64]{0,1:T(8,128)} %get-tuple-element.267) | copy-start | bytes 196612
  103.1 1.5 %copy-start.4 = (bf16[1,256,1,5,64]{4,1,3,2,0:T(8,128)(2,1)S(1)}, bf16[1,256,1,5,64]{4,1,3,2,0:T(8,128)(2,1)}, u32[]{:S(2)}) copy-start(bf16[1,256,1,5,64]{4,1,3,2,0:T(8,128)(2,1)} %copy-done.3) | copy-start | bytes 491524
  103.1 1.5 %copy-start.6 = (bf16[1,256,1,5,64]{4,1,3,2,0:T(8,128)(2,1)S(1)}, bf16[1,256,1,5,64]{4,1,3,2,0:T(8,128)(2,1)}, u32[]{:S(2)}) copy-start(bf16[1,256,1,5,64]{4,1,3,2,0:T(8,128)(2,1)} %copy-done.5) | copy-start | bytes 491524
  103.1 2.0 %copy-start.14 = (f32[256]{0:T(256)S(1)}, f32[256]{0:T(256)}, u32[]{:S(2)}) copy-start(f32[256]{0:T(256)} %copy-done.13) | copy-start | bytes 3076
  103.2 2.0 %copy-start.16 = (f32[64]{0:T(128)S(1)}, f32[64]{0:T(128)}, u32[]{:S(2)}) copy-start(f32[64]{0:T(128)} %copy-done.15) | copy-start | bytes 772
Sparse Core Ops, SparseCore 0:
  17.9 40.9 all-gather.1
  83.8 32.6 reduce-scatter.1
